TPU v7x, 256 devices: a whole 4x4x8 slice. The times are simulated.
256 devices in a mesh: row: 32 (over y, z), col: 8 (over x, core).
Axes of the slice: x: 4, y: 4, z: 8, core: 2. Of those that a mesh axis runs over, the one named last changes fastest.
Arguments:
- acts: bfloat16 [6144, 28672], P('col', 'row'), may hold values from -12 to 12
- out_grad: bfloat16 [6144, 8192], P('row', 'col'), may hold values from -12 to 12
- lengths: int32 [8], replicated, may hold values from 1 to 768, 4800 in all
Outputs:
- weight_grad: bfloat16 [28672, 8192], P('row', 'col')
- norms: float32 [8], replicated
All inputs are finite; a program needn't handle non-finite values.
Results may differ from a plain program's by a relative error of at most 0.0013.
Values may be sent and summed in bfloat16 or wider, within the bound.
No kernel may reach another device: no remote copies, remote signals or barrier semaphores. Data moves between devices by JAX's collectives and lax.ppermute only.
A program may use at most 128 MiB of HBM per device.

v0:
```python
import jax
import jax.numpy as jnp
from jax import lax
from jax.sharding import PartitionSpec as P

FF = 28672
D = 8192


def body(acts, out_grad, lengths):
    n_row = lax.axis_size("row")
    own_rows = out_grad.shape[0]
    tokens = own_rows * n_row
    seqs = lengths.shape[0]
    seq_len = tokens // seqs
    slot = lax.broadcasted_iota(jnp.int32, (seq_len, 1), 0)
    act_full = lax.all_gather(acts, "col", axis=0, tiled=True)
    grad_full = lax.all_gather(out_grad, "row", axis=0, tiled=True)
    products = []
    locals_ = []
    for seq in range(seqs):
        act_rows = act_full[seq * seq_len : (seq + 1) * seq_len]
        grad_rows = grad_full[seq * seq_len : (seq + 1) * seq_len]
        grad_rows = jnp.where(slot < lengths[seq], grad_rows, jnp.zeros_like(grad_rows))
        product = lax.dot_general(
            act_rows, grad_rows, (((0,), (0,)), ((), ())), preferred_element_type=jnp.float32
        )
        products.append(product)
        locals_.append(jnp.sum(product * product))
    squares = lax.psum(jnp.stack(locals_), ("row", "col"))
    divisor = float(FF) * float(D) * float(seq_len)
    norms = jnp.sqrt(squares / divisor)
    scale = 1.0 / (norms + 0.1)
    total = scale[0] * products[0]
    for seq in range(1, seqs):
        total = total + scale[seq] * products[seq]
    weight_grad = (total / jnp.sqrt(jnp.float32(tokens))).astype(jnp.bfloat16)
    return (weight_grad, norms)


def solution(mesh):
    placed = (P("col", "row"), P("row", "col"), P())
    return jax.shard_map(
        body, mesh=mesh, in_specs=placed, out_specs=(P("row", "col"), P()), check_vma=False
    )
```

profile of v0, /device:TPU:1, one launch (start us, length us, event | category | flops | bytes accessed | tf_op | source)
XLA Modules:
  0.0 344.8 jit_solution(8986895510977710011)
XLA Ops:
  7.2 0.0 all-gather.5.cloned.1.call-start
  7.2 0.7 all-gather.5.cloned.1.call-update
  7.9 0.0 all-gather.3.cloned.1.call-start
  7.9 0.7 all-gather.3.cloned.1.call-update
  8.6 1.6 fusion.42
  10.3 0.7 iota_compare_fusion.1
  10.9 0.7 iota_compare_fusion.2
  11.6 0.6 iota_compare_fusion.3
  12.2 0.7 iota_compare_fusion.4
  12.9 0.6 iota_compare_fusion.5
  13.5 0.6 iota_compare_fusion.6
  14.1 0.6 iota_compare_fusion.7
  14.8 0.6 iota_compare_fusion
  15.3 62.0 %all-gather.5.cloned.1.call-done = bf16[6144,896]{1,0:T(8,128)(2,1)} async-done(((bf16[768,896]{1,0:T(8,128)(2,1)}), bf16[6144,896]{1,0:T(8,128)(2,1)}) %all-gather.5.cloned.1.call-update) | async-done | bytes 11010064 | tf_op jit(solution)/shard_map/all_gather | solution.py:17
  77.3 121.9 %all-gather.3.cloned.1.call-done = bf16[6144,1024]{1,0:T(8,128)(2,1)} async-done(((bf16[192,1024]{1,0:T(8,128)(2,1)}), bf16[6144,1024]{1,0:T(8,128)(2,1)}) %all-gather.3.cloned.1.call-update) | async-done | bytes 12582928 | tf_op jit(solution)/shard_map/all_gather | solution.py:18
  199.2 0.0 copy-start
  199.2 6.4 %multiply_reduce_fusion = (f32[]{:T(128)}, f32[1024,896]{1,0:T(8,128)}) fusion(bf16[6144,896]{1,0:T(8,128)(2,1)} %all-gather.5.cloned.1.call-done, bf16[6144,1024]{1,0:T(8,128)(2,1)} %all-gather.3.cloned.1.call-done, pred[768]{0:T(1024)(128)(4,1)S(1)} %iota_compare_fusion), kind=kOutput, calls=%fused_computation.1 | convolution fusion | flops 1411907584 | bytes 6619908 | tf_op jit(solution)/shard_map/dot_general | solution.py:25
  205.6 0.4 copy-done
  206.0 0.0 copy-start.1
  206.0 5.9 %multiply_reduce_fusion.7 = (f32[]{:T(128)}, f32[1024,896]{1,0:T(8,128)}) fusion(bf16[6144,896]{1,0:T(8,128)(2,1)} %all-gather.5.cloned.1.call-done, bf16[6144,1024]{1,0:T(8,128)(2,1)S(1)} %copy-done, pred[768]{0:T(1024)(128)(4,1)S(1)} %iota_compare_fusion.7), kind=kOutput, calls=%fused_computation.8 | convolution fusion | flops 1411907584 | bytes 6620164 | tf_op jit(solution)/shard_map/dot_general | solution.py:25
  211.8 0.0 copy-done.1
  211.8 4.5 %multiply_reduce_fusion.6 = (f32[]{:T(128)}, f32[1024,896]{1,0:T(8,128)}) fusion(bf16[6144,896]{1,0:T(8,128)(2,1)S(1)} %copy-done.1, bf16[6144,1024]{1,0:T(8,128)(2,1)S(1)} %copy-done, pred[768]{0:T(1024)(128)(4,1)S(1)} %iota_compare_fusion.6), kind=kOutput, calls=%fused_computation.7 | convolution fusion | flops 1411907584 | bytes 6620164 | tf_op jit(solution)/shard_map/dot_general | solution.py:25
  216.3 4.5 %multiply_reduce_fusion.5 = (f32[]{:T(128)}, f32[1024,896]{1,0:T(8,128)}) fusion(bf16[6144,896]{1,0:T(8,128)(2,1)S(1)} %copy-done.1, bf16[6144,1024]{1,0:T(8,128)(2,1)S(1)} %copy-done, pred[768]{0:T(1024)(128)(4,1)S(1)} %iota_compare_fusion.5), kind=kOutput, calls=%fused_computation.6 | convolution fusion | flops 1411907584 | bytes 6620164 | tf_op jit(solution)/shard_map/dot_general | solution.py:25
  220.8 4.5 %multiply_reduce_fusion.4 = (f32[]{:T(128)}, f32[1024,896]{1,0:T(8,128)}) fusion(bf16[6144,896]{1,0:T(8,128)(2,1)S(1)} %copy-done.1, bf16[6144,1024]{1,0:T(8,128)(2,1)S(1)} %copy-done, pred[768]{0:T(1024)(128)(4,1)S(1)} %iota_compare_fusion.4), kind=kOutput, calls=%fused_computation.5 | convolution fusion | flops 1411907584 | bytes 6620164 | tf_op jit(solution)/shard_map/dot_general | solution.py:25
  225.3 4.4 %multiply_reduce_fusion.3 = (f32[]{:T(128)}, f32[1024,896]{1,0:T(8,128)}) fusion(bf16[6144,896]{1,0:T(8,128)(2,1)S(1)} %copy-done.1, bf16[6144,1024]{1,0:T(8,128)(2,1)S(1)} %copy-done, pred[768]{0:T(1024)(128)(4,1)S(1)} %iota_compare_fusion.3), kind=kOutput, calls=%fused_computation.4 | convolution fusion | flops 1411907584 | bytes 6620164 | tf_op jit(solution)/shard_map/dot_general | solution.py:25
  229.8 4.6 %multiply_reduce_fusion.2 = (f32[]{:T(128)}, f32[1024,896]{1,0:T(8,128)}) fusion(bf16[6144,896]{1,0:T(8,128)(2,1)S(1)} %copy-done.1, bf16[6144,1024]{1,0:T(8,128)(2,1)S(1)} %copy-done, pred[768]{0:T(1024)(128)(4,1)S(1)} %iota_compare_fusion.2), kind=kOutput, calls=%fused_computation.3 | convolution fusion | flops 1411907584 | bytes 6620164 | tf_op jit(solution)/shard_map/dot_general | solution.py:25
  234.4 4.5 %multiply_reduce_fusion.1 = (f32[]{:T(128)}, f32[1024,896]{1,0:T(8,128)}) fusion(bf16[6144,896]{1,0:T(8,128)(2,1)S(1)} %copy-done.1, bf16[6144,1024]{1,0:T(8,128)(2,1)S(1)} %copy-done, pred[768]{0:T(1024)(128)(4,1)S(1)} %iota_compare_fusion.1), kind=kOutput, calls=%fused_computation.2 | convolution fusion | flops 1411907584 | bytes 6620164 | tf_op jit(solution)/shard_map/dot_general | solution.py:25
  238.9 5.1 %stack.35 = f32[8]{0:T(128)S(1)} concatenate(f32[1]{0:T(128)} %bitcast.1, f32[1]{0:T(128)} %bitcast.3, f32[1]{0:T(128)} %bitcast.5, f32[1]{0:T(128)} %bitcast.7, f32[1]{0:T(128)} %bitcast.9, f32[1]{0:T(128)} %bitcast.11, f32[1]{0:T(128)} %bitcast.13, f32[1]{0:T(128)} %bitcast.15), dimensions={0} | concatenate | bytes 64 | tf_op jit(solution)/shard_map/stack | solution.py:30
  244.0 74.9 %psum.7 = f32[8]{0:T(128)S(1)} all-reduce(f32[8]{0:T(128)S(1)} %stack.35), channel_id=1, replica_groups=mesh['row'=32,'col'=8] {'row','col'}, use_global_device_ids=true, to_apply=%region_8.9 | all-reduce | flops 8 | bytes 64 | tf_op jit(solution)/shard_map/psum | solution.py:30
  318.9 0.5 add_divide_fusion
  319.5 0.7 fusion.41
  320.1 15.4 %fusion = bf16[896,1024]{0,1:T(8,128)(2,1)S(1)} fusion(f32[1024,896]{1,0:T(8,128)} %get-tuple-element.37, f32[]{:T(128)} %bitcast.23, f32[1024,896]{1,0:T(8,128)} %get-tuple-element.35, f32[]{:T(128)} %bitcast.22, f32[1024,896]{1,0:T(8,128)} %get-tuple-element.33, f32[]{:T(128)} %bitcast.21, f32[1024,896]{1,0:T(8,128)} %get-tuple-element.31, f32[]{:T(128)} %bitcast.20, ...), kind=kLoop, calls=%fused_computation.9 | loop fusion | flops 15597568 | bytes 31195168 | tf_op jit(solution)/shard_map/convert_element_type | solution.py:37
  335.6 2.4 copy.5
Async XLA Ops:
  7.2 70.2 %all-gather.5.cloned.1.call-start = ((), (), s32[]{:S(2)}) async-start(), calls=%async_computation.1 | async-start | bytes 12386304 | tf_op jit(solution)/shard_map/all_gather | solution.py:17
  7.9 191.3 %all-gather.3.cloned.1.call-start = ((), (), s32[]{:S(2)}) async-start(), calls=%async_computation | async-start | bytes 12976128 | tf_op jit(solution)/shard_map/all_gather | solution.py:18
  199.2 6.8 %copy-start = (bf16[6144,1024]{1,0:T(8,128)(2,1)S(1)}, bf16[6144,1024]{1,0:T(8,128)(2,1)}, u32[]{:S(2)}) copy-start(bf16[6144,1024]{1,0:T(8,128)(2,1)} %all-gather.3.cloned.1.call-done) | copy-start | bytes 37748740
  206.0 5.9 %copy-start.1 = (bf16[6144,896]{1,0:T(8,128)(2,1)S(1)}, bf16[6144,896]{1,0:T(8,128)(2,1)}, u32[]{:S(2)}) copy-start(bf16[6144,896]{1,0:T(8,128)(2,1)} %all-gather.5.cloned.1.call-done) | copy-start | bytes 33030148
Sparse Core Ops, SparseCore 0:
  9.8 67.4 all-gather.4
  79.9 119.2 all-gather.2
where the time goes:
time: 345 us
  waiting for transfers between devices  185 us (54%)
  blocking collectives  74.9 us (22%)
  matrix products  39.3 us (11%)
  other arithmetic  20.9 us (6%)
  between operations  14.1 us (4%)
  local copies, waits for them, and re-layouts  10.2 us (3%)
    all_gather x1, waiting for transfers between devices, body(): grad_full = lax.all_gather(out_grad, 'row', axis=0, tiled=True)  122 us
    psum x1, blocking collectives, body(): squares = lax.psum(jnp.stack(locals_), ('row', 'col'))  74.9 us
    all_gather x1, waiting for transfers between devices, body(): act_full = lax.all_gather(acts, 'col', axis=0, tiled=True)  62 us
    dot_general x8, matrix products, body(): lax.dot_general(act_rows, grad_rows, (((0,), (0,)), ((), ())), preferred_...  39.3 us
    convert_element_type x1, other arithmetic, body(): weight_grad = (total / jnp.sqrt(jnp.float32(tokens))).astype(jnp.bfloat16)  15.4 us
  transfers between devices with their start and end apart: 2, of which 2 were waited for; matrix products, arithmetic and copies ran while one was open for 2% of the time, Pallas kernels for 0%

commit v1 on v0

--- a/solution.py
+++ b/solution.py
@@ -14,7 +14,12 @@
     seqs = lengths.shape[0]
     seq_len = tokens // seqs
     slot = lax.broadcasted_iota(jnp.int32, (seq_len, 1), 0)
-    act_full = lax.all_gather(acts, "col", axis=0, tiled=True)
+    ring = [acts]
+    for hop in range(7):
+        ring.append(lax.ppermute(ring[-1], "col", [(dev, (dev + 1) % 8) for dev in range(8)]))
+    act_full = jnp.roll(
+        jnp.concatenate(ring[::-1], axis=0), (lax.axis_index("col") + 1) * ring[0].shape[0], axis=0
+    )
     grad_full = lax.all_gather(out_grad, "row", axis=0, tiled=True)
     products = []
     locals_ = []

time: 345 us -> 325 us (0.942)
  waiting for transfers between devices: 185 us -> 101 us
  local copies, waits for them, and re-layouts: 10.2 us -> 35.5 us
  starting transfers between devices: 0.08 us -> 17.5 us
  blocking collectives: 74.9 us -> 87.7 us
  matrix products: 39.3 us -> 45.2 us
    all_gather x1, waiting for transfers between devices: 122 us -> 0.01 us  [body(): grad_full = lax.all_gather(out_grad, 'row', axis=0, tiled=True)]
    ppermute x0 -> x7, waiting for transfers between devices: none -> 101 us  [body(): lax.ppermute(ring[-1], 'col', [(dev, (dev + 1) % 8) for dev in range(8)])]
    all_gather x1 -> x0, waiting for transfers between devices: 62 us -> none  [body(): act_full = lax.all_gather(acts, 'col', axis=0, tiled=True)]
    unnamed x5 -> x35, local copies, waits for them, and re-layouts: 2.84 us -> 26.9 us
    ppermute x0 -> x7, starting transfers between devices: none -> 17.5 us  [body(): lax.ppermute(ring[-1], 'col', [(dev, (dev + 1) % 8) for dev in range(8)])]
    psum x1, blocking collectives: 74.9 us -> 87.7 us  [body(): squares = lax.psum(jnp.stack(locals_), ('row', 'col'))]
    dot_general x8, matrix products: 39.3 us -> 45.2 us  [body(): lax.dot_general(act_rows, grad_rows, (((0,), (0,)), ((), ())), preferred_...]
  transfers between devices with their start and end apart: 2 -> 8, of which waited for: 2 -> 7; matrix products, arithmetic and copies ran while one was open for 2% -> 10% of each run, Pallas kernels for 0% -> 0%
where the time goes in v1:
time: 325 us
  waiting for transfers between devices  101 us (31%)
  blocking collectives  87.7 us (27%)
  matrix products  45.2 us (14%)
  local copies, waits for them, and re-layouts  35.5 us (11%)
  other arithmetic  23.1 us (7%)
  starting transfers between devices  17.5 us (5%)
  between operations  14.1 us (4%)
    ppermute x7, waiting for transfers between devices, body(): lax.ppermute(ring[-1], 'col', [(dev, (dev + 1) % 8) for dev in range(8)])  101 us
    psum x1, blocking collectives, body(): squares = lax.psum(jnp.stack(locals_), ('row', 'col'))  87.7 us
    dot_general x8, matrix products, body(): lax.dot_general(act_rows, grad_rows, (((0,), (0,)), ((), ())), preferred_...  45.2 us
    unnamed x35, local copies, waits for them, and re-layouts  26.9 us
    convert_element_type x1, other arithmetic, body(): weight_grad = (total / jnp.sqrt(jnp.float32(tokens))).astype(jnp.bfloat16)  17.6 us
    ppermute x7, starting transfers between devices, body(): lax.ppermute(ring[-1], 'col', [(dev, (dev + 1) % 8) for dev in range(8)])  17.5 us
  transfers between devices with their start and end apart: 8, of which 7 were waited for; matrix products, arithmetic and copies ran while one was open for 10% of the time, Pallas kernels for 0%

profile of v1, /device:TPU:1, one launch (start us, length us, event | category | flops | bytes accessed | tf_op | source)
XLA Modules:
  0.0 324.6 jit_solution(15030945668532102172)
XLA Ops:
  7.2 0.0 all-gather.2.cloned.1.call-start
  7.2 0.7 all-gather.2.cloned.1.call-update
  7.9 2.6 collective-permute-start
  10.5 15.6 %collective-permute-done = bf16[768,896]{1,0:T(8,128)(2,1)S(1)} collective-permute-done((bf16[768,896]{1,0:T(8,128)(2,1)}, bf16[768,896]{1,0:T(8,128)(2,1)S(1)}, u32[]{:S(2)}, u32[]{:S(2)}) %collective-permute-start) | collective-permute-done | bytes 1376288 | tf_op jit(solution)/shard_map/ppermute | solution.py:19
  26.1 2.4 collective-permute-start.1
  28.5 15.3 %collective-permute-done.1 = bf16[768,896]{1,0:T(8,128)(2,1)S(1)} collective-permute-done((bf16[768,896]{1,0:T(8,128)(2,1)S(1)}, bf16[768,896]{1,0:T(8,128)(2,1)S(1)}, u32[]{:S(2)}, u32[]{:S(2)}) %collective-permute-start.1) | collective-permute-done | bytes 1376288 | tf_op jit(solution)/shard_map/ppermute | solution.py:19
  43.7 2.5 collective-permute-start.2
  46.2 15.3 %collective-permute-done.2 = bf16[768,896]{1,0:T(8,128)(2,1)S(1)} collective-permute-done((bf16[768,896]{1,0:T(8,128)(2,1)S(1)}, bf16[768,896]{1,0:T(8,128)(2,1)S(1)}, u32[]{:S(2)}, u32[]{:S(2)}) %collective-permute-start.2) | collective-permute-done | bytes 1376288 | tf_op jit(solution)/shard_map/ppermute | solution.py:19
  61.4 1.1 copy-done.1
  62.5 2.5 collective-permute-start.3
  65.0 15.3 %collective-permute-done.3 = bf16[768,896]{1,0:T(8,128)(2,1)S(1)} collective-permute-done((bf16[768,896]{1,0:T(8,128)(2,1)S(1)}, bf16[768,896]{1,0:T(8,128)(2,1)S(1)}, u32[]{:S(2)}, u32[]{:S(2)}) %collective-permute-start.3) | collective-permute-done | bytes 1376288 | tf_op jit(solution)/shard_map/ppermute | solution.py:19
  80.3 1.1 copy-done.3
  81.3 2.5 collective-permute-start.4
  83.8 15.3 %collective-permute-done.4 = bf16[768,896]{1,0:T(8,128)(2,1)S(1)} collective-permute-done((bf16[768,896]{1,0:T(8,128)(2,1)S(1)}, bf16[768,896]{1,0:T(8,128)(2,1)S(1)}, u32[]{:S(2)}, u32[]{:S(2)}) %collective-permute-start.4) | collective-permute-done | bytes 1376288 | tf_op jit(solution)/shard_map/ppermute | solution.py:19
  99.1 1.1 copy-done.5
  100.1 2.5 collective-permute-start.5
  102.6 15.3 %collective-permute-done.5 = bf16[768,896]{1,0:T(8,128)(2,1)} collective-permute-done((bf16[768,896]{1,0:T(8,128)(2,1)S(1)}, bf16[768,896]{1,0:T(8,128)(2,1)}, u32[]{:S(2)}, u32[]{:S(2)}) %collective-permute-start.5) | collective-permute-done | bytes 1376288 | tf_op jit(solution)/shard_map/ppermute | solution.py:19
  117.9 2.6 collective-permute-start.6
  120.5 1.6 fusion.49
  122.1 0.6 iota_compare_fusion.2
  122.7 0.6 iota_compare_fusion.1
  123.2 0.6 iota_compare_fusion.6
  123.9 0.6 iota_compare_fusion.5
  124.5 0.6 iota_compare_fusion.4
  125.1 0.7 iota_compare_fusion.3
  125.8 0.7 iota_compare_fusion.7
  126.5 0.6 iota_compare_fusion
  127.1 0.0 copy-start.4
  127.1 8.9 %collective-permute-done.6 = bf16[768,896]{1,0:T(8,128)(2,1)} collective-permute-done((bf16[768,896]{1,0:T(8,128)(2,1)}, bf16[768,896]{1,0:T(8,128)(2,1)}, u32[]{:S(2)}, u32[]{:S(2)}) %collective-permute-start.6) | collective-permute-done | bytes 1376288 | tf_op jit(solution)/shard_map/ppermute | solution.py:19
  136.0 2.6 constant_dynamic-update-slice_fusion.15
  138.6 2.6 constant_dynamic-update-slice_fusion.14
  141.2 0.0 copy-done.6
  141.2 1.2 constant_dynamic-update-slice_fusion.13
  142.4 0.0 copy-done.4
  142.4 1.2 constant_dynamic-update-slice_fusion.12
  143.6 0.0 copy-done.2
  143.6 1.2 constant_dynamic-update-slice_fusion.11
  144.9 1.2 constant_dynamic-update-slice_fusion.10
  146.1 1.3 constant_dynamic-update-slice_fusion.9
  147.4 0.0 copy-done
  147.4 1.2 constant_dynamic-update-slice_fusion.8
  148.6 2.5 constant_dynamic-update-slice_fusion.7
  151.1 2.6 constant_dynamic-update-slice_fusion.6
  153.7 1.2 constant_dynamic-update-slice_fusion.5
  154.9 1.2 constant_dynamic-update-slice_fusion.4
  156.1 1.2 constant_dynamic-update-slice_fusion.3
  157.3 1.2 constant_dynamic-update-slice_fusion.2
  158.5 1.2 constant_dynamic-update-slice_fusion.1
  159.7 1.2 constant_dynamic-update-slice_fusion
  160.9 6.1 %multiply_reduce_fusion.7 = (f32[]{:T(128)}, f32[896,1024]{1,0:T(8,128)}) fusion(bf16[6144,1024]{1,0:T(8,128)(2,1)} %all-gather.2.cloned.1.call-done, pred[768]{0:T(1024)(128)(4,1)S(1)} %iota_compare_fusion.7, bf16[12288,896]{1,0:T(8,128)(2,1)} %constant_dynamic-update-slice_fusion, s32[]{:T(128)S(6)} %select_n.39), kind=kOutput, calls=%fused_computation.8 | convolution fusion | flops 1411907584 | bytes 6619912 | tf_op jit(solution)/shard_map/dot_general | solution.py:30
  167.1 6.1 %multiply_reduce_fusion.2 = (f32[]{:T(128)}, f32[896,1024]{1,0:T(8,128)}) fusion(bf16[6144,1024]{1,0:T(8,128)(2,1)} %all-gather.2.cloned.1.call-done, pred[768]{0:T(1024)(128)(4,1)S(1)} %iota_compare_fusion.2, bf16[12288,896]{1,0:T(8,128)(2,1)} %constant_dynamic-update-slice_fusion, s32[]{:T(128)S(6)} %add.54), kind=kOutput, calls=%fused_computation.3 | convolution fusion | flops 1411907584 | bytes 6619912 | tf_op jit(solution)/shard_map/dot_general | solution.py:30
  173.2 0.0 slice-done
  173.2 0.0 slice-done.1
  173.2 5.5 %multiply_reduce_fusion.1 = (f32[]{:T(128)}, f32[896,1024]{1,0:T(8,128)}) fusion(bf16[6144,1024]{1,0:T(8,128)(2,1)S(1)} %bitcast.25, pred[768]{0:T(1024)(128)(4,1)S(1)} %iota_compare_fusion.1, bf16[12288,896]{1,0:T(8,128)(2,1)} %constant_dynamic-update-slice_fusion, s32[]{:T(128)S(6)} %add.55), kind=kOutput, calls=%fused_computation.2 | convolution fusion | flops 1411907584 | bytes 6620168 | tf_op jit(solution)/shard_map/dot_general | solution.py:30
  178.7 5.5 %multiply_reduce_fusion.6 = (f32[]{:T(128)}, f32[896,1024]{1,0:T(8,128)}) fusion(bf16[6144,1024]{1,0:T(8,128)(2,1)S(1)} %bitcast.25, pred[768]{0:T(1024)(128)(4,1)S(1)} %iota_compare_fusion.6, bf16[12288,896]{1,0:T(8,128)(2,1)} %constant_dynamic-update-slice_fusion, s32[]{:T(128)S(6)} %add.50), kind=kOutput, calls=%fused_computation.7 | convolution fusion | flops 1411907584 | bytes 6620168 | tf_op jit(solution)/shard_map/dot_general | solution.py:30
  184.2 5.5 %multiply_reduce_fusion.5 = (f32[]{:T(128)}, f32[896,1024]{1,0:T(8,128)}) fusion(bf16[6144,1024]{1,0:T(8,128)(2,1)S(1)} %bitcast.25, pred[768]{0:T(1024)(128)(4,1)S(1)} %iota_compare_fusion.5, bf16[12288,896]{1,0:T(8,128)(2,1)} %constant_dynamic-update-slice_fusion, s32[]{:T(128)S(6)} %add.51), kind=kOutput, calls=%fused_computation.6 | convolution fusion | flops 1411907584 | bytes 6620168 | tf_op jit(solution)/shard_map/dot_general | solution.py:30
  189.7 5.6 %multiply_reduce_fusion.4 = (f32[]{:T(128)}, f32[896,1024]{1,0:T(8,128)}) fusion(bf16[6144,1024]{1,0:T(8,128)(2,1)S(1)} %bitcast.25, pred[768]{0:T(1024)(128)(4,1)S(1)} %iota_compare_fusion.4, bf16[12288,896]{1,0:T(8,128)(2,1)} %constant_dynamic-update-slice_fusion, s32[]{:T(128)S(6)} %add.52), kind=kOutput, calls=%fused_computation.5 | convolution fusion | flops 1411907584 | bytes 6620168 | tf_op jit(solution)/shard_map/dot_general | solution.py:30
  195.3 5.4 %multiply_reduce_fusion.3 = (f32[]{:T(128)}, f32[896,1024]{1,0:T(8,128)}) fusion(bf16[6144,1024]{1,0:T(8,128)(2,1)S(1)} %bitcast.25, pred[768]{0:T(1024)(128)(4,1)S(1)} %iota_compare_fusion.3, bf16[12288,896]{1,0:T(8,128)(2,1)} %constant_dynamic-update-slice_fusion, s32[]{:T(128)S(6)} %add.53), kind=kOutput, calls=%fused_computation.4 | convolution fusion | flops 1411907584 | bytes 6620168 | tf_op jit(solution)/shard_map/dot_general | solution.py:30
  200.7 5.5 %multiply_reduce_fusion = (f32[]{:T(128)}, f32[896,1024]{1,0:T(8,128)}) fusion(bf16[6144,1024]{1,0:T(8,128)(2,1)S(1)} %bitcast.25, pred[768]{0:T(1024)(128)(4,1)S(1)} %iota_compare_fusion, bf16[12288,896]{1,0:T(8,128)(2,1)} %constant_dynamic-update-slice_fusion, s32[]{:T(128)S(6)} %add.56), kind=kOutput, calls=%fused_computation.1 | convolution fusion | flops 1411907584 | bytes 6620168 | tf_op jit(solution)/shard_map/dot_general | solution.py:30
  206.2 5.1 %stack.35 = f32[8]{0:T(128)S(1)} concatenate(f32[1]{0:T(128)} %bitcast.1, f32[1]{0:T(128)} %bitcast.3, f32[1]{0:T(128)} %bitcast.5, f32[1]{0:T(128)} %bitcast.7, f32[1]{0:T(128)} %bitcast.9, f32[1]{0:T(128)} %bitcast.11, f32[1]{0:T(128)} %bitcast.13, f32[1]{0:T(128)} %bitcast.15), dimensions={0} | concatenate | bytes 64 | tf_op jit(solution)/shard_map/stack | solution.py:35
  211.2 87.7 %psum.7 = f32[8]{0:T(128)S(1)} all-reduce(f32[8]{0:T(128)S(1)} %stack.35), channel_id=1, replica_groups=mesh['row'=32,'col'=8] {'row','col'}, use_global_device_ids=true, to_apply=%region_8.9 | all-reduce | flops 8 | bytes 64 | tf_op jit(solution)/shard_map/psum | solution.py:35
  299.0 0.5 add_divide_fusion
  299.5 0.7 fusion.48
  300.2 17.6 %multiply_convert_fusion = bf16[896,1024]{1,0:T(8,128)(2,1)} fusion(f32[896,1024]{1,0:T(8,128)} %get-tuple-element.35, f32[896,1024]{1,0:T(8,128)} %get-tuple-element.33, f32[896,1024]{1,0:T(8,128)} %get-tuple-element.31, f32[896,1024]{1,0:T(8,128)} %get-tuple-element.29, f32[896,1024]{1,0:T(8,128)} %get-tuple-element.27, f32[896,1024]{1,0:T(8,128)} %get-tuple-element.25, ...), kind=kLoop, calls=%fused_computation | loop fusion | flops 15597568 | bytes 31195168 | tf_op jit(solution)/shard_map/convert_element_type | solution.py:42
  (12 shorter events, 0.0 us)
Async XLA Ops:
  7.2 153.8 %all-gather.2.cloned.1.call-start = ((), (), s32[]{:S(2)}) async-start(), calls=%async_computation | async-start | bytes 12976128 | tf_op jit(solution)/shard_map/all_gather | solution.py:23
  7.9 18.2 %collective-permute-start = (bf16[768,896]{1,0:T(8,128)(2,1)}, bf16[768,896]{1,0:T(8,128)(2,1)S(1)}, u32[]{:S(2)}, u32[]{:S(2)}) collective-permute-start(bf16[768,896]{1,0:T(8,128)(2,1)} %param.3), channel_id=1, source_target_pairs={{0,1},{1,2},{2,3},{3,4},{4,5},{5,6},{6,7},{7,0},{8,9},{9,10},{10,1... | collective-permute-start | bytes 4128776 | tf_op jit(solution)/shard_map/ppermute | solution.py:19
  26.1 17.6 %collective-permute-start.1 = (bf16[768,896]{1,0:T(8,128)(2,1)S(1)}, bf16[768,896]{1,0:T(8,128)(2,1)S(1)}, u32[]{:S(2)}, u32[]{:S(2)}) collective-permute-start(bf16[768,896]{1,0:T(8,128)(2,1)S(1)} %collective-permute-done), channel_id=1, source_target_pairs={{0,1},{1,2},{2,3},{3,4},{4,5},{5,6},{6,7},{7,0},{8,9},{9,10},{10,1... | collective-permute-start | bytes 4128776 | tf_op jit(solution)/shard_map/ppermute | solution.py:19
  43.7 17.7 %collective-permute-start.2 = (bf16[768,896]{1,0:T(8,128)(2,1)S(1)}, bf16[768,896]{1,0:T(8,128)(2,1)S(1)}, u32[]{:S(2)}, u32[]{:S(2)}) collective-permute-start(bf16[768,896]{1,0:T(8,128)(2,1)S(1)} %collective-permute-done.1), channel_id=1, source_target_pairs={{0,1},{1,2},{2,3},{3,4},{4,5},{5,6},{6,7},{7,0},{8,9},{9,10},{10,1... | collective-permute-start | bytes 4128776 | tf_op jit(solution)/shard_map/ppermute | solution.py:19
  61.4 1.1 copy-start.1
  62.5 17.7 %collective-permute-start.3 = (bf16[768,896]{1,0:T(8,128)(2,1)S(1)}, bf16[768,896]{1,0:T(8,128)(2,1)S(1)}, u32[]{:S(2)}, u32[]{:S(2)}) collective-permute-start(bf16[768,896]{1,0:T(8,128)(2,1)S(1)} %collective-permute-done.2), channel_id=1, source_target_pairs={{0,1},{1,2},{2,3},{3,4},{4,5},{5,6},{6,7},{7,0},{8,9},{9,10},{10,1... | collective-permute-start | bytes 4128776 | tf_op jit(solution)/shard_map/ppermute | solution.py:19
  80.3 1.1 copy-start.3
  81.3 17.7 %collective-permute-start.4 = (bf16[768,896]{1,0:T(8,128)(2,1)S(1)}, bf16[768,896]{1,0:T(8,128)(2,1)S(1)}, u32[]{:S(2)}, u32[]{:S(2)}) collective-permute-start(bf16[768,896]{1,0:T(8,128)(2,1)S(1)} %collective-permute-done.3), channel_id=1, source_target_pairs={{0,1},{1,2},{2,3},{3,4},{4,5},{5,6},{6,7},{7,0},{8,9},{9,10},{10,1... | collective-permute-start | bytes 4128776 | tf_op jit(solution)/shard_map/ppermute | solution.py:19
  99.1 1.1 copy-start.5
  100.1 17.7 %collective-permute-start.5 = (bf16[768,896]{1,0:T(8,128)(2,1)S(1)}, bf16[768,896]{1,0:T(8,128)(2,1)}, u32[]{:S(2)}, u32[]{:S(2)}) collective-permute-start(bf16[768,896]{1,0:T(8,128)(2,1)S(1)} %collective-permute-done.4), channel_id=1, source_target_pairs={{0,1},{1,2},{2,3},{3,4},{4,5},{5,6},{6,7},{7,0},{8,9},{9,10},{10,1... | collective-permute-start | bytes 4128776 | tf_op jit(solution)/shard_map/ppermute | solution.py:19
  117.9 18.2 %collective-permute-start.6 = (bf16[768,896]{1,0:T(8,128)(2,1)}, bf16[768,896]{1,0:T(8,128)(2,1)}, u32[]{:S(2)}, u32[]{:S(2)}) collective-permute-start(bf16[768,896]{1,0:T(8,128)(2,1)} %collective-permute-done.5), channel_id=1, source_target_pairs={{0,1},{1,2},{2,3},{3,4},{4,5},{5,6},{6,7},{7,0},{8,9},{9,10},{10,1... | collective-permute-start | bytes 4128776 | tf_op jit(solution)/shard_map/ppermute | solution.py:19
  120.5 20.8 %copy-start.6 = (bf16[768,896]{1,0:T(8,128)(2,1)S(1)}, bf16[768,896]{1,0:T(8,128)(2,1)}, u32[]{:S(2)}) copy-start(bf16[768,896]{1,0:T(8,128)(2,1)} %copy-done.5) | copy-start | bytes 4128772
  127.1 15.3 %copy-start.4 = (bf16[768,896]{1,0:T(8,128)(2,1)S(1)}, bf16[768,896]{1,0:T(8,128)(2,1)}, u32[]{:S(2)}) copy-start(bf16[768,896]{1,0:T(8,128)(2,1)} %copy-done.3) | copy-start | bytes 4128772
  138.6 5.0 %copy-start.2 = (bf16[768,896]{1,0:T(8,128)(2,1)S(1)}, bf16[768,896]{1,0:T(8,128)(2,1)}, u32[]{:S(2)}) copy-start(bf16[768,896]{1,0:T(8,128)(2,1)} %copy-done.1) | copy-start | bytes 4128772
  143.6 3.7 %copy-start = (bf16[768,896]{1,0:T(8,128)(2,1)S(1)}, bf16[768,896]{1,0:T(8,128)(2,1)}, u32[]{:S(2)}) copy-start(bf16[768,896]{1,0:T(8,128)(2,1)} %param.3) | copy-start | bytes 4128772
  160.9 12.2 %slice-start = ((s8[12582912]{0:T(1024)(128)(4,1)}), s8[4194304]{0:T(1024)(128)(4,1)S(1)}, s32[]{:S(2)}) async-start(s8[12582912]{0:T(1024)(128)(4,1)} %bitcast.24), calls=%async_computation.1 | async-start | bytes 8388608
  160.9 12.2 %slice-start.1 = ((s8[12582912]{0:T(1024)(128)(4,1)}), s8[4194304]{0:T(1024)(128)(4,1)S(1)}, s32[]{:S(2)}) async-start(s8[12582912]{0:T(1024)(128)(4,1)} %bitcast.24), calls=%async_computation.2 | async-start | bytes 8388608
  167.1 6.1 %slice-start.2 = ((s8[12582912]{0:T(1024)(128)(4,1)}), s8[4194304]{0:T(1024)(128)(4,1)S(1)}, s32[]{:S(2)}) async-start(s8[12582912]{0:T(1024)(128)(4,1)} %bitcast.24), calls=%async_computation.3 | async-start | bytes 8388608
Sparse Core Ops, SparseCore 0:
  10.6 123.1 all-gather.1
